TPU v7x, 256 devices: a whole 4x4x8 slice. The times are simulated.
256 devices in a mesh: grp: 16 (over x_lo, z), blk: 16 (over x_hi, y, core).
Axes of the slice: x: 4 (x_hi: 2, x_lo: 2; x = x_hi * 2 + x_lo), y: 4, z: 8, core: 2. Of those that a mesh axis runs over, the one named last changes fastest.
Arguments:
- raw_ints: bfloat16 [2048, 256, 512], P('grp', 'blk'), may hold values from -0.59765625 to 0.59765625
- metric: bfloat16 [2048, 2048], P(None, 'grp'), as said below
- occ_energy: float32 [256], replicated, may hold values from -2 to -0.3
- virt_energy: float32 [512], replicated, may hold values from 0.2 to 5
Outputs:
- density: float32 [2048, 256, 512], P(None, ('blk', 'grp'))
- pair_energy: float32 [256, 4], P(('blk', 'grp'))
Inputs may be any that keep to these rules, and one draw needn't show every extreme that they name: `metric`: Symmetric.
All inputs are finite; a program needn't handle non-finite values.
Results may differ from a plain program's by a relative error of at most 0.0033.
Values may be sent and summed in bfloat16 or wider, within the bound.
A program may use at most 128 MiB of HBM per device.

v0:
```python
import jax
import jax.numpy as jnp
from jax import lax
from jax.sharding import PartitionSpec as P

VISITS = 4


def swapped(value, axis, bit):
    mask = 2**bit
    pairs = [(source, source ^ mask) for source in range(lax.axis_size(axis))]
    return lax.ppermute(value, axis, pairs)


def passed_along(block, axis, distance):
    devices = range(lax.axis_size(axis))
    route = [((i - distance) % len(devices), i) for i in devices]
    return lax.ppermute(block, axis, route)


def pair_terms(own, other, e_own, e_other, virt_energy):
    coulomb = lax.dot_general(
        own, other, (((0,), (0,)), ((), ())), preferred_element_type=jnp.float32
    )
    denom = e_own + e_other - virt_energy[:, None] - virt_energy[None, :]
    amplitude = coulomb / denom
    tilde = 2.0 * amplitude - amplitude.T
    energy = jnp.sum(coulomb * tilde)
    tilde_low = tilde.astype(jnp.bfloat16)
    contrib = lax.dot_general(
        other, tilde_low, (((1,), (1,)), ((), ())), preferred_element_type=jnp.float32
    )
    return (contrib, energy)


def local(raw_ints, metric, occ_energy, virt_energy):
    n_grp = lax.axis_size("grp")
    n_blk = lax.axis_size("blk")
    total_dev = n_grp * n_blk
    moved = lax.all_to_all(raw_ints, "grp", split_axis=1, concat_axis=0, tiled=True)
    own_raw = moved.reshape(moved.shape[0], moved.shape[2])
    own = jnp.dot(
        lax.all_gather(metric, "grp", axis=1, tiled=True),
        own_raw,
        preferred_element_type=jnp.float32,
    ).astype(jnp.bfloat16)
    place = lax.axis_index("grp") * n_blk + lax.axis_index("blk")

    def orbital_at(where_at):
        return where_at % n_blk * n_grp + where_at // n_blk

    e_own = lax.dynamic_index_in_dim(occ_energy, orbital_at(place), 0, keepdims=False)
    density, energy = pair_terms(own, own, e_own, e_own, virt_energy)
    energies = [energy]
    traveller = own
    for step in range(1, VISITS):
        partner = jnp.where(
            (place - step) % 2 == 0, (place - step) % total_dev, (place + step) % total_dev
        )
        if step % 2 == 1:
            traveller = swapped(traveller, ("grp", "blk"), 0)
        else:
            shifted = passed_along(traveller, ("grp", "blk"), 1)
            paired = swapped(shifted, ("grp", "blk"), 0)
            traveller = passed_along(paired, ("grp", "blk"), -1)
        e_other = lax.dynamic_index_in_dim(occ_energy, orbital_at(partner), 0, keepdims=False)
        contrib, energy = pair_terms(own, traveller, e_own, e_other, virt_energy)
        density = density + contrib
        energies.append(energy)
    return (density[:, None, :], jnp.stack(energies)[None, :])


def solution(mesh):
    in_specs = (P("grp", "blk", None), P(None, "grp"), P(), P())
    out_specs = (P(None, ("blk", "grp"), None), P(("blk", "grp"), None))
    return jax.shard_map(local, mesh=mesh, in_specs=in_specs, out_specs=out_specs, check_vma=False)
```

profile of v0, /device:TPU:1, one launch (start us, length us, event | category | flops | bytes accessed | tf_op | source)
XLA Modules:
  0.0 311.1 jit_solution(17193218113815496922)
XLA Ops:
  7.2 0.0 all-gather.2.cloned.1.call-start
  7.2 0.7 all-gather.2.cloned.1.call-update
  7.9 2.8 copy.11
  10.7 71.3 %all_to_all.15 = bf16[128,16,512]{2,0,1:T(8,128)(2,1)S(1)} all-to-all(bf16[128,16,512]{2,0,1:T(8,128)(2,1)S(1)} %copy.11), channel_id=1, replica_groups=mesh['grp'=16,'blk'=16] {'grp'}, dimensions={1} | all-to-all | bytes 4194304 | tf_op jit(solution)/shard_map/all_to_all | solution.py:40
  82.0 88.1 %all-gather.2.cloned.1.call-done = bf16[2048,2048]{1,0:T(8,128)(2,1)} async-done(((bf16[2048,128]{1,0:T(8,128)(2,1)}), bf16[2048,2048]{1,0:T(8,128)(2,1)}) %all-gather.2.cloned.1.call-update) | async-done | bytes 8388624 | tf_op jit(solution)/shard_map/all_gather | solution.py:43
  170.1 8.1 %convolution_convert_fusion = bf16[2048,512]{1,0:T(8,128)(2,1)S(1)} fusion(bf16[2048,2048]{1,0:T(8,128)(2,1)} %all-gather.2.cloned.1.call-done, bf16[2048,512]{1,0:T(8,128)(2,1)S(1)} %bitcast.67), kind=kOutput, calls=%fused_computation.1 | convolution fusion | flops 4296015872 | bytes 12582912 | tf_op jit(solution)/shard_map/dot_general | solution.py:42
  178.2 0.0 copy-start.9
  178.2 1.4 copy-done.9
  179.6 6.9 %collective-permute-start = (bf16[2048,512]{1,0:T(8,128)(2,1)S(1)}, bf16[2048,512]{1,0:T(8,128)(2,1)S(1)}, u32[]{:S(2)}, u32[]{:S(2)}) collective-permute-start(bf16[2048,512]{1,0:T(8,128)(2,1)S(1)} %convolution_convert_fusion), channel_id=1, source_target_pairs={{0,1},{1,0},{2,3},{3,2},{4,5},{5,4},{6,7},{7,6},{8,9},{9,8},{10,11... | collective-permute-start | bytes 6291464 | tf_op jit(solution)/shard_map/ppermute | solution.py:12
  186.5 3.8 %collective-permute-done = bf16[2048,512]{1,0:T(8,128)(2,1)S(1)} collective-permute-done((bf16[2048,512]{1,0:T(8,128)(2,1)S(1)}, bf16[2048,512]{1,0:T(8,128)(2,1)S(1)}, u32[]{:S(2)}, u32[]{:S(2)}) %collective-permute-start) | collective-permute-done | bytes 2097184 | tf_op jit(solution)/shard_map/ppermute | solution.py:12
  190.3 1.3 copy-done.13
  191.6 1.6 collective-permute-start.1
  193.1 23.0 %collective-permute-done.1 = bf16[2048,512]{1,0:T(8,128)(2,1)S(1)} collective-permute-done((bf16[2048,512]{1,0:T(8,128)(2,1)S(1)}, bf16[2048,512]{1,0:T(8,128)(2,1)S(1)}, u32[]{:S(2)}, u32[]{:S(2)}) %collective-permute-start.1) | collective-permute-done | bytes 2097184 | tf_op jit(solution)/shard_map/ppermute | solution.py:18
  216.1 6.7 %collective-permute-start.2 = (bf16[2048,512]{1,0:T(8,128)(2,1)S(1)}, bf16[2048,512]{1,0:T(8,128)(2,1)}, u32[]{:S(2)}, u32[]{:S(2)}) collective-permute-start(bf16[2048,512]{1,0:T(8,128)(2,1)S(1)} %collective-permute-done.1), channel_id=1, source_target_pairs={{0,1},{1,0},{2,3},{3,2},{4,5},{5,4},{6,7},{7,6},{8,9},{9,8},{10,11... | collective-permute-start | bytes 6291464 | tf_op jit(solution)/shard_map/ppermute | solution.py:12
  222.8 3.9 %collective-permute-done.2 = bf16[2048,512]{1,0:T(8,128)(2,1)} collective-permute-done((bf16[2048,512]{1,0:T(8,128)(2,1)S(1)}, bf16[2048,512]{1,0:T(8,128)(2,1)}, u32[]{:S(2)}, u32[]{:S(2)}) %collective-permute-start.2) | collective-permute-done | bytes 2097184 | tf_op jit(solution)/shard_map/ppermute | solution.py:12
  226.8 0.4 collective-permute-start.3
  227.1 0.0 copy-done.8
  227.1 0.6 fusion.15
  232.4 0.0 copy-done.7
  232.4 3.5 %fusion.16 = f32[512,512]{1,0:T(8,128)S(1)} fusion(bf16[2048,512]{1,0:T(8,128)(2,1)} %copy-done.9), kind=kOutput, calls=%fused_computation.27 | convolution fusion | flops 1073741824 | bytes 3145728 | tf_op jit(solution)/shard_map/dot_general | solution.py:22
  235.9 0.3 copy.12
  236.2 0.0 copy-start.2
  236.2 16.3 %collective-permute-done.3 = bf16[2048,512]{1,0:T(8,128)(2,1)} collective-permute-done((bf16[2048,512]{1,0:T(8,128)(2,1)}, bf16[2048,512]{1,0:T(8,128)(2,1)}, u32[]{:S(2)}, u32[]{:S(2)}) %collective-permute-start.3) | collective-permute-done | bytes 2097184 | tf_op jit(solution)/shard_map/ppermute | solution.py:18
  252.5 0.2 collective-permute-start.4
  252.7 5.3 %fusion.9 = f32[2048,512]{1,0:T(8,128)} fusion(bf16[2048,512]{1,0:T(8,128)(2,1)} %copy-done.9, f32[512,512]{0,1:T(8,128)S(1)} %copy.12, f32[512,512]{1,0:T(8,128)S(1)} %fusion.16, f32[512]{0:T(512)S(1)} %copy-done.7, f32[512]{0:T(512)S(1)} %get-tuple-element.12), kind=kOutput, calls=%fused_computation.19 | convolution fusion | flops 1075576832 | bytes 8392704 | tf_op jit(solution)/shard_map/dot_general | solution.py:30
  258.1 0.0 copy-done.2
  258.1 0.0 copy-done.10
  258.1 0.0 copy-done.14
  258.1 1.3 fusion.17
  259.3 0.0 copy-start.3
  259.3 0.3 copy.13
  259.7 0.0 copy-start.4
  259.7 0.0 copy-start.11
  259.7 5.6 %fusion.7 = f32[2048,512]{1,0:T(8,128)} fusion(bf16[2048,512]{1,0:T(8,128)(2,1)} %copy-done.13, f32[512,512]{0,1:T(8,128)S(1)} %copy.13, f32[512,512]{1,0:T(8,128)S(1)} %fusion.17, f32[512]{0:T(512)S(1)} %get-tuple-element.11, f32[512]{0:T(512)S(1)} %copy-done.7), kind=kOutput, calls=%fused_computation.17 | convolution fusion | flops 1075576832 | bytes 8392704 | tf_op jit(solution)/shard_map/dot_general | solution.py:30
  265.3 0.0 copy-done.3
  265.3 0.0 copy-done.4
  265.3 0.0 copy-done.11
  265.3 3.9 %fusion.18 = f32[512,512]{1,0:T(8,128)} fusion(bf16[2048,512]{1,0:T(8,128)(2,1)S(1)} %copy-done.11, bf16[2048,512]{1,0:T(8,128)(2,1)} %collective-permute-done.3), kind=kOutput, calls=%fused_computation.29 | convolution fusion | flops 1073741824 | bytes 5242880 | tf_op jit(solution)/shard_map/dot_general | solution.py:22
  269.2 1.6 copy.14
  270.9 5.6 %fusion.5 = f32[2048,512]{1,0:T(8,128)} fusion(bf16[2048,512]{1,0:T(8,128)(2,1)} %collective-permute-done.3, f32[512,512]{0,1:T(8,128)S(1)} %copy.14, f32[512,512]{1,0:T(8,128)S(1)} %copy-done.5, f32[512]{0:T(512)S(1)} %get-tuple-element.13, f32[512]{0:T(512)S(1)} %copy-done.7), kind=kOutput, calls=%fused_computation.15 | convolution fusion | flops 1075576832 | bytes 8392704 | tf_op jit(solution)/shard_map/dot_general | solution.py:30
  276.5 0.0 collective-permute-done.4
  276.5 2.9 fusion.19
  279.4 0.3 copy.15
  279.7 4.4 %multiply_reduce_fusion.3 = (f32[]{:T(128)}, f32[]{:T(128)}, f32[]{:T(128)}, f32[]{:T(128)}) fusion(f32[512,512]{1,0:T(8,128)S(1)} %fusion.16, f32[512]{0:T(512)S(1)} %copy-done.7, f32[512]{0:T(512)S(1)} %get-tuple-element.12, f32[512,512]{0,1:T(8,128)} %copy-done.2, f32[512,512]{1,0:T(8,128)S(1)} %fusion.19, f32[512]{0:T(512)S(1)} %get-tuple-element.10, ...), kind=kLoop, calls=%fused_computation.13 | loop fusion | flops 8388604 | bytes 8398864 | tf_op jit(solution)/shard_map/reduce_sum | solution.py:28
  284.2 0.6 copy-done.1
  284.8 4.9 %add_bitcast_fusion = f32[2048,1,512]{2,0,1:T(8,128)S(1)} fusion(f32[2048,512]{1,0:T(8,128)} %fusion.5, f32[2048,512]{1,0:T(8,128)S(1)} %copy-done, f32[2048,512]{1,0:T(8,128)S(1)} %copy-done.1, bf16[2048,512]{1,0:T(8,128)(2,1)} %collective-permute-done.4, f32[512,512]{0,1:T(8,128)S(1)} %copy.15, f32[512,512]{1,0:T(8,128)S(1)} %fusion.19, ...), kind=kOutput, calls=%fused_computation | convolution fusion | flops 1078722560 | bytes 20975616 | tf_op jit(solution)/shard_map/dot_general | solution.py:30
  289.7 11.7 %copy.16 = f32[2048,1,512]{2,1,0:T(1,128)} copy(f32[2048,1,512]{2,0,1:T(8,128)S(1)} %add_bitcast_fusion) | data formatting | bytes 8388608
  301.4 2.9 maximum_bitcast_fusion
  (15 shorter events, 0.0 us)
Async XLA Ops:
  7.2 162.9 %all-gather.2.cloned.1.call-start = ((), (), s32[]{:S(2)}) async-start(), calls=%async_computation.1 | async-start | bytes 8912896 | tf_op jit(solution)/shard_map/all_gather | solution.py:43
  170.1 57.0 %copy-start.8 = (f32[256]{0:T(256)S(1)}, f32[256]{0:T(256)}, u32[]{:S(2)}) copy-start(f32[256]{0:T(256)} %param.6) | copy-start | bytes 3076
  170.1 62.3 %copy-start.7 = (f32[512]{0:T(512)S(1)}, f32[512]{0:T(512)}, u32[]{:S(2)}) copy-start(f32[512]{0:T(512)} %param.7) | copy-start | bytes 6148
  178.2 1.4 copy-start.9
  179.6 10.6 %collective-permute-start = (bf16[2048,512]{1,0:T(8,128)(2,1)S(1)}, bf16[2048,512]{1,0:T(8,128)(2,1)S(1)}, u32[]{:S(2)}, u32[]{:S(2)}) collective-permute-start(bf16[2048,512]{1,0:T(8,128)(2,1)S(1)} %convolution_convert_fusion), channel_id=1, source_target_pairs={{0,1},{1,0},{2,3},{3,2},{4,5},{5,4},{6,7},{7,6},{8,9},{9,8},{10,11... | collective-permute-start | bytes 6291464 | tf_op jit(solution)/shard_map/ppermute | solution.py:12
  190.3 1.3 copy-start.13
  191.6 24.5 %collective-permute-start.1 = (bf16[2048,512]{1,0:T(8,128)(2,1)S(1)}, bf16[2048,512]{1,0:T(8,128)(2,1)S(1)}, u32[]{:S(2)}, u32[]{:S(2)}) collective-permute-start(bf16[2048,512]{1,0:T(8,128)(2,1)S(1)} %collective-permute-done), channel_id=1, source_target_pairs={{255,0},{0,1},{1,2},{2,3},{3,4},{4,5},{5,6},{6,7},{7,8},{8,9},{9,1... | collective-permute-start | bytes 6291464 | tf_op jit(solution)/shard_map/ppermute | solution.py:18
  216.1 10.6 %collective-permute-start.2 = (bf16[2048,512]{1,0:T(8,128)(2,1)S(1)}, bf16[2048,512]{1,0:T(8,128)(2,1)}, u32[]{:S(2)}, u32[]{:S(2)}) collective-permute-start(bf16[2048,512]{1,0:T(8,128)(2,1)S(1)} %collective-permute-done.1), channel_id=1, source_target_pairs={{0,1},{1,0},{2,3},{3,2},{4,5},{5,4},{6,7},{7,6},{8,9},{9,8},{10,11... | collective-permute-start | bytes 6291464 | tf_op jit(solution)/shard_map/ppermute | solution.py:12
  226.8 25.8 %collective-permute-start.3 = (bf16[2048,512]{1,0:T(8,128)(2,1)}, bf16[2048,512]{1,0:T(8,128)(2,1)}, u32[]{:S(2)}, u32[]{:S(2)}) collective-permute-start(bf16[2048,512]{1,0:T(8,128)(2,1)} %collective-permute-done.2), channel_id=1, source_target_pairs={{1,0},{2,1},{3,2},{4,3},{5,4},{6,5},{7,6},{8,7},{9,8},{10,9},{11,1... | collective-permute-start | bytes 6291464 | tf_op jit(solution)/shard_map/ppermute | solution.py:18
  236.2 21.8 %copy-start.2 = (f32[512,512]{0,1:T(8,128)}, f32[512,512]{0,1:T(8,128)S(1)}, u32[]{:S(2)}) copy-start(f32[512,512]{0,1:T(8,128)S(1)} %copy.12) | copy-start | bytes 3145732
  252.5 24.0 %collective-permute-start.4 = (bf16[2048,512]{1,0:T(8,128)(2,1)}, bf16[2048,512]{1,0:T(8,128)(2,1)}, u32[]{:S(2)}, u32[]{:S(2)}) collective-permute-start(bf16[2048,512]{1,0:T(8,128)(2,1)} %collective-permute-done.3), channel_id=1, source_target_pairs={{0,1},{1,0},{2,3},{3,2},{4,5},{5,4},{6,7},{7,6},{8,9},{9,8},{10,11... | collective-permute-start | bytes 6291464 | tf_op jit(solution)/shard_map/ppermute | solution.py:12
  252.7 5.3 %copy-start.10 = (bf16[2048,512]{1,0:T(8,128)(2,1)S(1)}, bf16[2048,512]{1,0:T(8,128)(2,1)}, u32[]{:S(2)}) copy-start(bf16[2048,512]{1,0:T(8,128)(2,1)} %copy-done.9) | copy-start | bytes 6291460
  252.7 5.3 %copy-start.14 = (bf16[2048,512]{1,0:T(8,128)(2,1)S(1)}, bf16[2048,512]{1,0:T(8,128)(2,1)}, u32[]{:S(2)}) copy-start(bf16[2048,512]{1,0:T(8,128)(2,1)} %copy-done.13) | copy-start | bytes 6291460
  259.3 6.0 %copy-start.3 = (f32[512,512]{1,0:T(8,128)}, f32[512,512]{1,0:T(8,128)S(1)}, u32[]{:S(2)}) copy-start(f32[512,512]{1,0:T(8,128)S(1)} %fusion.17) | copy-start | bytes 3145732
  259.7 5.6 %copy-start.4 = (f32[512,512]{0,1:T(8,128)}, f32[512,512]{0,1:T(8,128)S(1)}, u32[]{:S(2)}) copy-start(f32[512,512]{0,1:T(8,128)S(1)} %copy.13) | copy-start | bytes 3145732
  259.7 5.6 %copy-start.11 = (bf16[2048,512]{1,0:T(8,128)(2,1)S(1)}, bf16[2048,512]{1,0:T(8,128)(2,1)}, u32[]{:S(2)}) copy-start(bf16[2048,512]{1,0:T(8,128)(2,1)} %copy-done.9) | copy-start | bytes 6291460
  269.2 1.7 copy-start.5
  270.8 5.7 %copy-start.6 = (f32[512,512]{0,1:T(8,128)}, f32[512,512]{0,1:T(8,128)S(1)}, u32[]{:S(2)}) copy-start(f32[512,512]{0,1:T(8,128)S(1)} %copy.14) | copy-start | bytes 3145732
  270.9 5.7 %copy-start.12 = (bf16[2048,512]{1,0:T(8,128)(2,1)S(1)}, bf16[2048,512]{1,0:T(8,128)(2,1)}, u32[]{:S(2)}) copy-start(bf16[2048,512]{1,0:T(8,128)(2,1)} %copy-done.9) | copy-start | bytes 6291460
  279.7 4.4 %copy-start = (f32[2048,512]{1,0:T(8,128)S(1)}, f32[2048,512]{1,0:T(8,128)}, u32[]{:S(2)}) copy-start(f32[2048,512]{1,0:T(8,128)} %fusion.9) | copy-start | bytes 12582916
  279.7 5.0 %copy-start.1 = (f32[2048,512]{1,0:T(8,128)S(1)}, f32[2048,512]{1,0:T(8,128)}, u32[]{:S(2)}) copy-start(f32[2048,512]{1,0:T(8,128)} %fusion.7) | copy-start | bytes 12582916
Sparse Core Ops, SparseCore 0:
  9.7 160.3 all-gather.1
where the time goes:
time: 312 us; the launch traced here: 311 us
  waiting for transfers between devices  136 us (44%)
  blocking collectives  71.3 us (23%)
  matrix products  41.1 us (13%)
  local copies, waits for them, and re-layouts  21 us (7%)
  between operations  18.8 us (6%)
  starting transfers between devices  15.8 us (5%)
  other arithmetic  7.37 us (2%)
    all_gather x1, waiting for transfers between devices, local(): lax.all_gather(metric, 'grp', axis=1, tiled=True)  88.1 us
    all_to_all x1, blocking collectives, local(): lax.all_to_all(raw_ints, 'grp', split_axis=1, concat_axis=0, tiled=True)  71.3 us
    ppermute x2, waiting for transfers between devices, passed_along(): return lax.ppermute(block, axis, route)  39.3 us
    dot_general x4, matrix products, pair_terms(): lax.dot_general(other, tilde_low, (((1,), (1,)), ((), ())), preferred_ele...  21.5 us
    unnamed x32, local copies, waits for them, and re-layouts  17.8 us
    ppermute x3, starting transfers between devices, swapped(): return lax.ppermute(value, axis, pairs)  13.8 us
    dot_general x4, matrix products, pair_terms(): lax.dot_general(own, other, (((0,), (0,)), ((), ())), preferred_element_t...  11.5 us
    dot_general x1, matrix products, local(): jnp.dot(lax.all_gather(metric, 'grp', axis=1, tiled=True), own_raw, prefe...  8.13 us
  transfers between devices with their start and end apart: 6, of which 5 were waited for; matrix products, arithmetic and copies ran while one was open for 10% of the time, Pallas kernels for 0%

commit v1 on v0

v1 whole, which is shorter than its diff:
```python
import functools

import jax
import jax.numpy as jnp
from jax import lax
from jax.experimental import pallas as pl
from jax.experimental.pallas import tpu as pltpu
from jax.sharding import PartitionSpec as P

VISITS = 4
NAUX = 2048
NV = 512
CHUNKS = 4
WIDE = NV // CHUNKS
MESH = pl.DeviceIdType.MESH
F32 = jnp.float32
BF16 = jnp.bfloat16


def device(xl, z, xh, y, c):
    return (xl * 8 + z, xh * 8 + y * 2 + c)


def kernel(
    raw, metric, occ, virt, out_hbm, energy_out,
    send, owned, full, mine, sib, near, far, mine_t, coul, amp, vsum, tlow, rows,
    a2a_s, a2a_r, m1_s, m1_r, mx_s, mx_r, my_s, my_r, xy_s, xy_r, yx_s, yx_r,
    sw_s, sw_r, sib_s, sib_r, vis_s, vis_r, far_s, far_r, out_s,
):
    g = lax.axis_index("grp")
    b = lax.axis_index("blk")
    xl, z = g // 8, g % 8
    xh, y, c = b // 8, (b // 2) % 4, b % 2
    x = xh * 2 + xl
    other = (g, b + 1 - 2 * c)
    chip = g * 8 + xh * 4 + y
    ahead = (chip + 1 - 2 * c) % 128
    behind = (chip + 127 + 2 * c) % 128

    def chip_core(n):
        return (n // 8, (n % 8) * 2 + c)

    def at_x(d):
        x2 = (x + d) % 4
        return device(x2 % 2, z, x2 // 2, y, c)

    def at_y(d):
        return device(xl, z, xh, (y + d) % 4, c)

    def at_g(d):
        return ((g + d) % 16, b)

    def at_z(d):
        return (xl * 8 + (z + d) % 8, b)

    barrier = pltpu.get_barrier_semaphore()
    partners = [at_g(d) for d in range(1, 16)]
    partners += [at_x(d) for d in range(1, 4)] + [at_y(d) for d in range(1, 4)]
    partners += [other, chip_core(ahead), chip_core(behind)]
    for partner in partners:
        pl.semaphore_signal(barrier, inc=1, device_id=partner, device_id_type=MESH)

    order = lax.broadcasted_iota(jnp.int32, (256, 256), 0)
    column = lax.broadcasted_iota(jnp.int32, (256, 256), 1)
    swap = jnp.where(column == (order % 16) * 16 + order // 16, 1.0, 0.0).astype(BF16)

    pl.semaphore_wait(barrier, len(partners))

    sends = []

    def push(src, dst, ssem, rsem, to):
        copy = pltpu.make_async_remote_copy(
            src_ref=src, dst_ref=dst, send_sem=ssem, recv_sem=rsem,
            device_id=to, device_id_type=MESH,
        )
        copy.start()
        sends.append(copy)

    def arrived(ref, sem):
        pltpu.make_async_copy(ref, ref, sem).wait()

    part = c * 8 + xh * 4 + y
    part_rows = pl.ds(pl.multiple_of(part * 128, 128), 128)
    own_columns = pl.ds(pl.multiple_of(g * 128, 128), 128)
    for d in range(1, 8):
        push(metric.at[part_rows, :], full.at[part_rows, own_columns], m1_s.at[d], m1_r, at_z(d))
    pltpu.make_async_copy(metric.at[part_rows, :], full.at[part_rows, own_columns], m1_r).start()

    def relayout(k, carry):
        at = pl.multiple_of(k * 256, 256)
        moved = jnp.dot(swap, raw[pl.ds(at, 256), :], preferred_element_type=F32).astype(BF16)
        to = pl.multiple_of(k * 16, 16)
        for i in range(16):
            send[i, pl.ds(to, 16), :] = moved[i * 16:(i + 1) * 16, :]
        return carry

    lax.fori_loop(0, 8, relayout, 0)

    land = pl.ds(pl.multiple_of(g * 128, 128), 128)
    for k in range(CHUNKS):
        cut = slice(k * WIDE, (k + 1) * WIDE)
        pltpu.make_async_copy(send.at[g, :, cut], owned.at[land, cut], a2a_r.at[k]).start()
        for d in range(1, 16):
            to = at_g(d)
            push(send.at[to[0], :, cut], owned.at[land, cut], a2a_s.at[k, d], a2a_r.at[k], to)

    def piece(px, py, half):
        hi, lo = px // 2, px % 2
        at = pl.multiple_of((c * 8 + hi * 4 + py) * 128, 128)
        col = pl.multiple_of(lo * 1024 + half * 512, 512)
        return full.at[pl.ds(at, 128), pl.ds(col, 512)]

    def from_x(d):
        return (x + 4 - d) % 4

    def from_y(d):
        return (y + 4 - d) % 4

    arrived(full.at[part_rows, pl.ds(0, 1024)], m1_r)
    for d in (1, 3, 2):
        push(piece(x, y, 0), piece(x, y, 0), mx_s.at[d], mx_r.at[d], at_x(d))
        push(piece(x, y, 1), piece(x, y, 1), my_s.at[d], my_r.at[d], at_y(d))
    for d in (1, 3, 2):
        push(piece(x, y, 0), piece(x, y, 0), xy_s.at[0, d], xy_r.at[d], at_y(d))
        push(piece(x, y, 1), piece(x, y, 1), yx_s.at[0, d], yx_r.at[d], at_x(d))
    for e in (1, 3, 2):
        arrived(piece(x, y, 0), mx_r.at[e])
        for d in (1, 3, 2):
            p = piece(from_x(e), y, 0)
            push(p, p, xy_s.at[e, d], xy_r.at[d], at_y(d))
        arrived(piece(x, y, 1), my_r.at[e])
        for d in (1, 3, 2):
            p = piece(x, from_y(e), 1)
            push(p, p, yx_s.at[e, d], yx_r.at[d], at_x(d))
    core_rows = pl.ds(pl.multiple_of(c * 1024, 1024), 1024)
    for d in (1, 3, 2):
        arrived(full.at[pl.ds(0, 512), pl.ds(0, 512)], xy_r.at[d])
    for lo in range(2):
        p = full.at[core_rows, pl.ds(lo * 1024, 512)]
        push(p, p, sw_s.at[lo], sw_r, other)
    for d in (1, 3, 2):
        arrived(full.at[pl.ds(0, 512), pl.ds(0, 512)], yx_r.at[d])
    for lo in range(2):
        p = full.at[core_rows, pl.ds(lo * 1024 + 512, 512)]
        push(p, p, sw_s.at[2 + lo], sw_r, other)

    wide = jnp.broadcast_to(virt[...], (512, 512))
    vsum[...] = wide + wide.T

    arrived(full.at[core_rows, :], sw_r)

    for k in range(CHUNKS):
        cut = slice(k * WIDE, (k + 1) * WIDE)
        arrived(owned.at[:, cut], a2a_r.at[k])

        def fit(q, carry, cut=cut):
            at = pl.ds(pl.multiple_of(q * 256, 256), 256)
            fitted = jnp.dot(full[at, :], owned[:, cut], preferred_element_type=F32)
            mine[at, cut] = fitted.astype(BF16)
            mine_t[cut, at] = fitted.T.astype(BF16)
            return carry

        lax.fori_loop(0, 8, fit, 0)
        push(mine.at[:, cut], near.at[:, cut], vis_s.at[k], vis_r.at[k], chip_core(ahead))
        push(mine.at[:, cut], sib.at[:, cut], sib_s.at[k], sib_r.at[k], other)

    def orbital(p):
        return (p % 16) * 16 + p // 16

    place = g * 16 + b
    e_own = occ[orbital(place)]

    def partner(s):
        if s == 0:
            return place
        even = (place + 256 - s) % 2 == 0
        return jnp.where(even, place + 256 - s, place + s) % 256

    energies = []

    def terms(s, fit_of):
        e_sum = e_own + occ[orbital(partner(s))]

        def product(r, carry):
            at = pl.ds(pl.multiple_of(r * 128, 128), 128)
            value = jnp.dot(mine_t[at, :], fit_of[...], preferred_element_type=F32)
            coul[at, :] = value
            amp[at, :] = value / (e_sum - vsum[at, :])
            return carry

        lax.fori_loop(0, 4, product, 0)

        total = jnp.zeros((128, 512), F32)
        for r in range(4):
            at = slice(r * 128, (r + 1) * 128)
            straight = amp[at, :]
            turned = amp[:, at].T
            total = total + coul[at, :] * (2.0 * straight - turned)
            tlow[s * 512 + r * 128:s * 512 + (r + 1) * 128, :] = (
                2.0 * turned - straight
            ).astype(BF16)
        energies.append(jnp.sum(total))

    terms(0, mine)
    for k in range(CHUNKS):
        cut = slice(k * WIDE, (k + 1) * WIDE)
        arrived(near.at[:, cut], vis_r.at[k])
        push(near.at[:, cut], far.at[:, cut], far_s.at[k], far_r.at[k], other)
    for k in range(CHUNKS):
        arrived(sib.at[:, k * WIDE:(k + 1) * WIDE], sib_r.at[k])
    terms(1, sib)
    terms(2, near)
    for k in range(CHUNKS):
        arrived(far.at[:, k * WIDE:(k + 1) * WIDE], far_r.at[k])
    terms(3, far)

    def dense(q, carry):
        at = pl.ds(pl.multiple_of(q * 256, 256), 256)
        value = jnp.dot(mine[at, :], tlow[0:512, :], preferred_element_type=F32)
        value += jnp.dot(sib[at, :], tlow[512:1024, :], preferred_element_type=F32)
        value += jnp.dot(near[at, :], tlow[1024:1536, :], preferred_element_type=F32)
        value += jnp.dot(far[at, :], tlow[1536:2048, :], preferred_element_type=F32)
        for t in range(4):
            rows[pl.ds(q * 1024 + t, 256, stride=4), :] = value[:, t * 128:(t + 1) * 128]
        lines = pl.ds(pl.multiple_of(q * 1024, 1024), 1024)
        pltpu.make_async_copy(rows.at[lines, :], out_hbm.at[lines, :], out_s).start()
        return carry

    lax.fori_loop(0, 8, dense, 0)

    lane = lax.broadcasted_iota(jnp.int32, (1, VISITS), 1)
    listed = jnp.zeros((1, VISITS), F32)
    for s in range(VISITS):
        listed = jnp.where(lane == s, energies[s], listed)
    energy_out[...] = listed

    for copy in sends:
        copy.wait_send()
    pltpu.make_async_copy(rows, out_hbm, out_s).wait()


def local(raw_ints, metric, occ_energy, virt_energy):
    dma = pltpu.SemaphoreType.DMA
    vmem = pl.BlockSpec(memory_space=pltpu.VMEM)
    hbm = pl.BlockSpec(memory_space=pl.ANY)
    density, energy = pl.pallas_call(
        kernel,
        out_shape=(
            jax.ShapeDtypeStruct((NAUX * NV // 128, 128), F32),
            jax.ShapeDtypeStruct((1, VISITS), F32),
        ),
        in_specs=[vmem, hbm, pl.BlockSpec(memory_space=pltpu.SMEM), vmem],
        out_specs=(hbm, vmem),
        scratch_shapes=[
            pltpu.VMEM((16, 128, NV), BF16),
            pltpu.VMEM((NAUX, NV), BF16),
            pltpu.VMEM((NAUX, NAUX), BF16),
            pltpu.VMEM((NAUX, NV), BF16),
            pltpu.VMEM((NAUX, NV), BF16),
            pltpu.VMEM((NAUX, NV), BF16),
            pltpu.VMEM((NAUX, NV), BF16),
            pltpu.VMEM((NV, NAUX), BF16),
            pltpu.VMEM((NV, NV), F32),
            pltpu.VMEM((NV, NV), F32),
            pltpu.VMEM((NV, NV), F32),
            pltpu.VMEM((VISITS * NV, NV), BF16),
            pltpu.VMEM((NAUX * NV // 128, 128), F32),
            dma((CHUNKS, 16)), dma((CHUNKS,)),
            dma((8,)), dma(()),
            dma((4,)), dma((4,)),
            dma((4,)), dma((4,)),
            dma((4, 4)), dma((4,)),
            dma((4, 4)), dma((4,)),
            dma((4,)), dma(()),
            dma((CHUNKS,)), dma((CHUNKS,)),
            dma((CHUNKS,)), dma((CHUNKS,)),
            dma((CHUNKS,)), dma((CHUNKS,)),
            dma(()),
        ],
        compiler_params=pltpu.CompilerParams(
            collective_id=0, has_side_effects=True, vmem_limit_bytes=56 << 20
        ),
        name="pair_rows",
    )(raw_ints.reshape(NAUX, NV), metric, occ_energy, virt_energy.reshape(1, NV))
    return density.reshape(NAUX, 1, NV), energy


def solution(mesh):
    in_specs = (P("grp", "blk", None), P(None, "grp"), P(), P())
    out_specs = (P(None, ("blk", "grp"), None), P(("blk", "grp"), None))
    return jax.shard_map(local, mesh=mesh, in_specs=in_specs, out_specs=out_specs, check_vma=False)
```

time: 312 us -> 126 us (0.40)
  waiting for transfers between devices: 136 us -> 0 us
  Pallas kernels: 0 us -> 116 us
  blocking collectives: 71.3 us -> 0 us
  matrix products: 41.1 us -> 0 us
  between operations: 18.8 us -> 0.65 us
  starting transfers between devices: 15.8 us -> 0 us
  local copies, waits for them, and re-layouts: 21 us -> 8.22 us
  other arithmetic: 7.37 us -> 0 us
    pallas_call x0 -> x1, Pallas kernels: none -> 116 us  [local(): pl.pallas_call(kernel, out_shape=(jax.ShapeDtypeStruct((NAUX * NV // 128,...]
    all_gather x1 -> x0, waiting for transfers between devices: 88.1 us -> none  [local(): lax.all_gather(metric, 'grp', axis=1, tiled=True)]
    all_to_all x1 -> x0, blocking collectives: 71.3 us -> none  [local(): lax.all_to_all(raw_ints, 'grp', split_axis=1, concat_axis=0, tiled=True)]
    ppermute x5 -> x0, waiting for transfers between devices: 47 us -> none  [the longest x2 39.3 us: passed_along(): return lax.ppermute(block, axis, route)]
    dot_general x9 -> x0, matrix products: 41.1 us -> none  [the longest x4 21.5 us: pair_terms(): lax.dot_general(other, tilde_low, (((1,), (1,)), ((), ())), preferred_ele...]
    ppermute x5 -> x0, starting transfers between devices: 15.7 us -> none  [the longest x3 13.8 us: swapped(): return lax.ppermute(value, axis, pairs)]
    unnamed x32 -> x4, local copies, waits for them, and re-layouts: 17.8 us -> 8.22 us
    reduce_sum x1 -> x0, other arithmetic: 4.42 us -> none  [pair_terms(): energy = jnp.sum(coulomb * tilde)]
  transfers between devices with their start and end apart: 6 -> 0, of which waited for: 5 -> 0; matrix products, arithmetic and copies ran while one was open for 10% -> 0% of each run, Pallas kernels for 0% -> 0%
where the time goes in v1:
time: 126 us; the launch traced here: 125 us
  Pallas kernels  116 us (92%)
  local copies, waits for them, and re-layouts  8.22 us (7%)
    pallas_call x1, Pallas kernels, local(): pl.pallas_call(kernel, out_shape=(jax.ShapeDtypeStruct((NAUX * NV // 128,...  116 us
    unnamed x4, local copies, waits for them, and re-layouts  8.22 us

profile of v1, /device:TPU:1, one launch (start us, length us, event | category | flops | bytes accessed | tf_op | source)
XLA Modules:
  0.0 125.3 jit_solution(8624974089301527121)
XLA Ops:
  0.6 116.5 %pair_rows.1 = (f32[8192,128]{1,0:T(8,128)}, f32[1,4]{1,0:T(1,128)}) custom-call(bf16[2048,512]{1,0:T(8,128)(2,1)} %bitcast.4, bf16[2048,128]{1,0:T(8,128)(2,1)} %metric.1, f32[256]{0:T(256)} %occ.1, f32[1,512]{1,0:T(1,128)} %bitcast.5), custom_call_target="tpu_custom_call" | custom-call | tf_op jit(solution)/shard_map/pair_rows/pallas_call | solution.py:246
  117.1 0.0 copy-start
  117.1 7.7 %copy.9 = f32[2048,1,512]{2,1,0:T(1,128)} copy(f32[2048,1,512]{2,1,0:T(1,128)} %bitcast.3) | data formatting | bytes 8388608
  124.8 0.0 copy-done
  124.8 0.5 copy.10
Async XLA Ops:
  117.1 7.7 %copy-start = (f32[1,4]{1,0:T(1,128)S(1)}, f32[1,4]{1,0:T(1,128)}, u32[]{:S(2)}) copy-start(f32[1,4]{1,0:T(1,128)} %get-tuple-element.11) | copy-start | bytes 52

commit v2 on v0

v2 whole, which is shorter than its diff:
```python
import jax
import jax.numpy as jnp
from jax import lax
from jax.experimental import pallas as pl
from jax.experimental.pallas import tpu as pltpu
from jax.sharding import PartitionSpec as P

VISITS = 4
NAUX = 2048
NV = 512
CUTS = ((0, 256), (256, 128), (384, 128))
SLOT = 72
MESH = pl.DeviceIdType.MESH
F32 = jnp.float32
BF16 = jnp.bfloat16


def device(xl, z, xh, y, c):
    return (xl * 8 + z, xh * 8 + y * 2 + c)


def pair_kernel(
    raw, metric, occ, virt, mine_out, sib_out, near_out, far_out, tlow_out, energy_out,
    send, owned, slots, full, mine, sib, near, far, mine_t, coul, amp, vsum, tlow,
    a2a_s, a2a_r, m1_s, m1_r, mx_s, mx_r, up_s, up_r, down_s, down_r, relay_s, relay_r,
    sw_s, sw_r, sib_s, sib_r, vis_s, vis_r, far_s, far_r, out_s,
):
    g = lax.axis_index("grp")
    b = lax.axis_index("blk")
    xl, z = g // 8, g % 8
    xh, y, c = b // 8, (b // 2) % 4, b % 2
    x = xh * 2 + xl
    other = (g, b + 1 - 2 * c)
    chip = g * 8 + xh * 4 + y
    ahead = (chip + 1 - 2 * c + 128) % 128
    behind = (chip + 127 + 2 * c) % 128

    def chip_core(n):
        return (n // 8, (n % 8) * 2 + c)

    def at_x(d):
        x2 = (x + d) % 4
        return device(x2 % 2, z, x2 // 2, y, c)

    def at_y(d):
        return device(xl, z, xh, (y + d) % 4, c)

    def at_g(d):
        return ((g + d) % 16, b)

    def at_z(d):
        return (xl * 8 + (z + d) % 8, b)

    barrier = pltpu.get_barrier_semaphore()
    partners = [at_g(d) for d in range(1, 16)]
    partners += [at_x(d) for d in range(1, 4)] + [at_y(d) for d in range(1, 4)]
    partners += [other, chip_core(ahead), chip_core(behind)]
    for partner in partners:
        pl.semaphore_signal(barrier, inc=1, device_id=partner, device_id_type=MESH)

    order = lax.broadcasted_iota(jnp.int32, (256, 256), 0)
    column = lax.broadcasted_iota(jnp.int32, (256, 256), 1)
    swap = jnp.where(column == (order % 16) * 16 + order // 16, 1.0, 0.0).astype(BF16)

    def relayout(k, carry):
        at = pl.multiple_of(k * 256, 256)
        moved = jnp.dot(swap, raw[pl.ds(at, 256), :], preferred_element_type=F32).astype(BF16)
        to = pl.multiple_of(k * 16, 16)
        for i in range(16):
            send[i, pl.ds(to, 16), :] = moved[i * 16:(i + 1) * 16, :]
        return carry

    lax.fori_loop(0, 8, relayout, 0)

    pl.semaphore_wait(barrier, len(partners))

    sends = []

    def push(src, dst, ssem, rsem, to):
        copy = pltpu.make_async_remote_copy(
            src_ref=src, dst_ref=dst, send_sem=ssem, recv_sem=rsem,
            device_id=to, device_id_type=MESH,
        )
        copy.start()
        sends.append(copy)

    def arrived(ref, sem):
        pltpu.make_async_copy(ref, ref, sem).wait()

    t = c * 8 + y * 2 + xh
    mine_columns = pl.ds(pl.multiple_of(g * 128, 128), 128)
    main_rows = pl.ds(pl.multiple_of((g * 128 + t * 64) % 2048, 64), 64)
    last_rows = pl.ds(pl.multiple_of((g * 128 + 1024 + t * 8) % 2048, 8), 8)
    parts = (
        (metric.at[main_rows, :], slots.at[t, pl.ds(0, 64), mine_columns]),
        (metric.at[last_rows, :], slots.at[t, pl.ds(64, 8), mine_columns]),
    )
    for d in (4, 3, 5, 2, 6, 1, 7):
        for h, (src, dst) in enumerate(parts):
            push(src, dst, m1_s.at[d, h], m1_r, at_z(d))
    for src, dst in parts:
        pltpu.make_async_copy(src, dst, m1_r).start()

    land = pl.ds(pl.multiple_of(g * 128, 128), 128)
    for k, (lo, wide) in enumerate(CUTS):
        cut = pl.ds(lo, wide)
        pltpu.make_async_copy(send.at[g, :, cut], owned.at[land, cut], a2a_r.at[k]).start()
        for d in range(1, 16):
            to = at_g(d)
            push(send.at[to[0], :, cut], owned.at[land, cut], a2a_s.at[k, d], a2a_r.at[k], to)

    def piece(py, e):
        px = (x + 4 - e) % 4
        at = c * 8 + py * 2 + px // 2
        return slots.at[at, :, pl.ds(pl.multiple_of((px % 2) * 1024, 1024), 1024)]

    below, above = (y + 3) % 4, (y + 1) % 4

    def spread(e):
        p = piece(y, e)
        push(p, p, up_s.at[e], up_r.at[e], at_y(1))
        push(p, p, down_s.at[e], down_r.at[e], at_y(3))

    def hand_over(py, k):
        p = slots.at[pl.ds(c * 8 + py * 2, 2), :, :]
        push(p, p, sw_s.at[k], sw_r, other)

    def relay_up(e):
        p = piece(below, e)
        arrived(p, up_r.at[e])
        push(p, p, relay_s.at[e], relay_r.at[e], at_y(1))

    def relay_down(e):
        p = piece(above, e)
        arrived(p, down_r.at[e])
        push(p, p, relay_s.at[e], relay_r.at[e], at_y(3))

    arrived(slots.at[t, :, pl.ds(0, 1024)], m1_r)
    for d in (1, 3, 2):
        push(piece(y, 0), piece(y, 0), mx_s.at[d], mx_r.at[d], at_x(d))
    spread(0)
    arrived(piece(y, 1), mx_r.at[1])
    spread(1)
    relay_up(0)
    arrived(piece(y, 3), mx_r.at[3])
    spread(3)
    relay_up(1)
    arrived(piece(y, 2), mx_r.at[2])
    spread(2)
    hand_over(y, 0)
    relay_down(3)
    arrived(piece(below, 3), up_r.at[3])
    arrived(piece(above, 0), down_r.at[0])
    arrived(piece(above, 1), down_r.at[1])
    relay_down(2)
    hand_over(above, 1)
    arrived(piece(below, 2), up_r.at[2])
    hand_over(below, 2)
    opposite = (y + 2) % 4
    for e in (0, 1, 3, 2):
        arrived(piece(opposite, e), relay_r.at[e])
    hand_over(opposite, 3)

    broad = jnp.broadcast_to(virt[...], (NV, NV))
    vsum[...] = broad + broad.T

    arrived(slots.at[pl.ds(0, 8), :, :], sw_r)

    def unfold(j, carry):
        column = pl.ds(pl.multiple_of(j * 128, 128), 128)

        def block(d, carry):
            i = (j + d) % 16
            row = pl.ds(pl.multiple_of(i * 128, 128), 128)
            value = slots[pl.ds(2 * d, 2), 0:64, column].reshape(128, 128)
            full[row, column] = value
            full[column, row] = value.T
            return carry

        lax.fori_loop(0, 8, block, 0, unroll=True)
        row = pl.ds(pl.multiple_of(((j + 8) % 16) * 128, 128), 128)
        value = slots[:, 64:72, column].astype(F32).reshape(128, 128)
        full[row, column] = value.astype(BF16)
        return carry

    lax.fori_loop(0, 16, unfold, 0)

    stores = []

    def keep(src, dst, n):
        copy = pltpu.make_async_copy(src, dst, out_s.at[n])
        copy.start()
        stores.append(copy)

    def visitor(k):
        cut = pl.ds(*CUTS[k])
        arrived(near.at[:, cut], vis_r.at[k])
        push(near.at[:, cut], far.at[:, cut], far_s.at[k], far_r.at[k], other)

    for k, (lo, wide) in enumerate(CUTS):
        cut = pl.ds(lo, wide)
        arrived(owned.at[:, cut], a2a_r.at[k])

        def fit(q, carry, cut=cut):
            at = pl.ds(pl.multiple_of(q * 1024, 1024), 1024)
            mine[at, cut] = jnp.dot(
                full[at, :], owned[:, cut], preferred_element_type=F32
            ).astype(BF16)
            return carry

        lax.fori_loop(0, 2, fit, 0)
        push(mine.at[:, cut], near.at[:, cut], vis_s.at[k], vis_r.at[k], chip_core(ahead))
        push(mine.at[:, cut], sib.at[:, cut], sib_s.at[k], sib_r.at[k], other)

        def turn(q, carry, lo=lo, wide=wide):
            at = pl.ds(pl.multiple_of(q * 256, 256), 256)
            mine_t[pl.ds(lo, wide), at] = mine[at, pl.ds(lo, wide)].T
            return carry

        lax.fori_loop(0, 8, turn, 0)
        if k == 1:
            visitor(0)
    keep(mine, mine_out, 0)

    def orbital(p):
        return (p % 16) * 16 + p // 16

    place = g * 16 + b
    e_own = occ[orbital(place)]

    def partner(s):
        if s == 0:
            return place
        even = (place + 256 - s) % 2 == 0
        return jnp.where(even, place + 256 - s, place + s) % 256

    def product(s, fit_of, lo, wide):
        cut = pl.ds(lo, wide)
        e_sum = e_own + occ[orbital(partner(s))]
        value = jnp.dot(mine_t[...], fit_of[:, cut], preferred_element_type=F32)
        coul[s, :, cut] = value
        amp[s, :, cut] = value / (e_sum - vsum[:, cut])

    energies = []

    def finish(s):
        total = jnp.zeros((128, NV), F32)
        for r in range(4):
            at = pl.ds(r * 128, 128)
            straight = amp[s, at, :]
            turned = amp[s, :, at].T
            total = total + coul[s, at, :] * (2.0 * straight - turned)
            tlow[pl.ds(s * NV + r * 128, 128), :] = (2.0 * turned - straight).astype(BF16)
        energies.append(jnp.sum(total))
        rows = pl.ds(s * NV, NV)
        keep(tlow.at[rows, :], tlow_out.at[rows, :], 4 + s)

    product(0, mine, 0, NV)
    finish(0)
    visitor(1)
    for k, (lo, wide) in enumerate(CUTS):
        arrived(sib.at[:, pl.ds(lo, wide)], sib_r.at[k])
    keep(sib, sib_out, 1)
    product(1, sib, 0, NV)
    finish(1)
    for k in (0, 1):
        product(2, near, *CUTS[k])
    for k in (0, 1):
        arrived(far.at[:, pl.ds(*CUTS[k])], far_r.at[k])
        product(3, far, *CUTS[k])
    visitor(2)
    keep(near, near_out, 2)
    product(2, near, *CUTS[2])
    finish(2)
    arrived(far.at[:, pl.ds(*CUTS[2])], far_r.at[2])
    keep(far, far_out, 3)
    product(3, far, *CUTS[2])
    finish(3)

    lane = lax.broadcasted_iota(jnp.int32, (1, VISITS), 1)
    listed = jnp.zeros((1, VISITS), F32)
    for s in range(VISITS):
        listed = jnp.where(lane == s, energies[s], listed)
    energy_out[...] = listed

    for copy in sends:
        copy.wait_send()
    for copy in stores:
        copy.wait()


def density_kernel(mine, sib, near, far, tlow, energy, out, energy_out):
    value = jnp.dot(mine[...], tlow[0:512, :], preferred_element_type=F32)
    value += jnp.dot(sib[...], tlow[512:1024, :], preferred_element_type=F32)
    value += jnp.dot(near[...], tlow[1024:1536, :], preferred_element_type=F32)
    value += jnp.dot(far[...], tlow[1536:2048, :], preferred_element_type=F32)
    for n in range(4):
        out[pl.ds(n, value.shape[0], stride=4), :] = value[:, n * 128:(n + 1) * 128]
    energy_out[...] = energy[...]


def local(raw_ints, metric, occ_energy, virt_energy):
    dma = pltpu.SemaphoreType.DMA
    vmem = pl.BlockSpec(memory_space=pltpu.VMEM)
    hbm = pl.BlockSpec(memory_space=pl.ANY)
    n = len(CUTS)
    fits = jax.ShapeDtypeStruct((NAUX, NV), BF16)
    fitted = pltpu.VMEM((NAUX, NV), BF16)
    mine, sib, near, far, tlow, energy = pl.pallas_call(
        pair_kernel,
        out_shape=(
            fits, fits, fits, fits,
            jax.ShapeDtypeStruct((VISITS * NV, NV), BF16),
            jax.ShapeDtypeStruct((1, VISITS), F32),
        ),
        in_specs=[vmem, hbm, pl.BlockSpec(memory_space=pltpu.SMEM), vmem],
        out_specs=(hbm, hbm, hbm, hbm, hbm, vmem),
        scratch_shapes=[
            pltpu.VMEM((16, 128, NV), BF16),
            fitted,
            pltpu.VMEM((16, SLOT, NAUX), BF16),
            pltpu.VMEM((NAUX, NAUX), BF16),
            fitted, fitted, fitted, fitted,
            pltpu.VMEM((NV, NAUX), BF16),
            pltpu.VMEM((VISITS, NV, NV), F32),
            pltpu.VMEM((VISITS, NV, NV), F32),
            pltpu.VMEM((NV, NV), F32),
            pltpu.VMEM((VISITS * NV, NV), BF16),
            dma((n, 16)), dma((n,)),
            dma((8, 2)), dma(()),
            dma((4,)), dma((4,)),
            dma((4,)), dma((4,)),
            dma((4,)), dma((4,)),
            dma((4,)), dma((4,)),
            dma((4,)), dma(()),
            dma((n,)), dma((n,)),
            dma((n,)), dma((n,)),
            dma((n,)), dma((n,)),
            dma((8,)),
        ],
        compiler_params=pltpu.CompilerParams(
            collective_id=0, has_side_effects=True, vmem_limit_bytes=56 << 20
        ),
        name="pair_terms",
    )(raw_ints.reshape(NAUX, NV), metric, occ_energy, virt_energy.reshape(1, NV))

    rows = 512
    part = pl.BlockSpec((rows, NV), lambda q: (q, 0))
    small = pl.BlockSpec((1, VISITS), lambda q: (0, 0))
    density, energy = pl.pallas_call(
        density_kernel,
        grid=(NAUX // rows,),
        out_shape=(
            jax.ShapeDtypeStruct((NAUX * NV // 128, 128), F32),
            jax.ShapeDtypeStruct((1, VISITS), F32),
        ),
        in_specs=[part, part, part, part, pl.BlockSpec((NAUX, NV), lambda q: (0, 0)), small],
        out_specs=(pl.BlockSpec((rows * 4, 128), lambda q: (q, 0)), small),
        compiler_params=pltpu.CompilerParams(vmem_limit_bytes=60 << 20),
        name="density_rows",
    )(mine, sib, near, far, tlow, energy)
    return density.reshape(NAUX, 1, NV), energy


def solution(mesh):
    in_specs = (P("grp", "blk", None), P(None, "grp"), P(), P())
    out_specs = (P(None, ("blk", "grp"), None), P(("blk", "grp"), None))
    return jax.shard_map(local, mesh=mesh, in_specs=in_specs, out_specs=out_specs, check_vma=False)
```

time: 312 us -> 103 us (0.33)
  waiting for transfers between devices: 136 us -> 0 us
  Pallas kernels: 0 us -> 102 us
  blocking collectives: 71.3 us -> 0 us
  matrix products: 41.1 us -> 0 us
  local copies, waits for them, and re-layouts: 21 us -> 0 us
  between operations: 18.8 us -> 0.64 us
  starting transfers between devices: 15.8 us -> 0 us
  other arithmetic: 7.37 us -> 0 us
    pallas_call x0 -> x2, Pallas kernels: none -> 102 us  [the longest x1 92.7 us: local(): pl.pallas_call(pair_kernel, out_shape=(fits, fits, fits, fits, jax.ShapeD...]
    all_gather x1 -> x0, waiting for transfers between devices: 88.1 us -> none  [local(): lax.all_gather(metric, 'grp', axis=1, tiled=True)]
    all_to_all x1 -> x0, blocking collectives: 71.3 us -> none  [local(): lax.all_to_all(raw_ints, 'grp', split_axis=1, concat_axis=0, tiled=True)]
    ppermute x5 -> x0, waiting for transfers between devices: 47 us -> none  [the longest x2 39.3 us: passed_along(): return lax.ppermute(block, axis, route)]
    dot_general x9 -> x0, matrix products: 41.1 us -> none  [the longest x4 21.5 us: pair_terms(): lax.dot_general(other, tilde_low, (((1,), (1,)), ((), ())), preferred_ele...]
    unnamed x32 -> x0, local copies, waits for them, and re-layouts: 17.8 us -> none
    ppermute x5 -> x0, starting transfers between devices: 15.7 us -> none  [the longest x3 13.8 us: swapped(): return lax.ppermute(value, axis, pairs)]
    reduce_sum x1 -> x0, other arithmetic: 4.42 us -> none  [pair_terms(): energy = jnp.sum(coulomb * tilde)]
  transfers between devices with their start and end apart: 6 -> 0, of which waited for: 5 -> 0; matrix products, arithmetic and copies ran while one was open for 10% -> 0% of each run, Pallas kernels for 0% -> 0%
where the time goes in v2:
time: 103 us
  Pallas kernels  102 us (99%)
    pallas_call x1, Pallas kernels, local(): pl.pallas_call(pair_kernel, out_shape=(fits, fits, fits, fits, jax.ShapeD...  92.7 us
    pallas_call x1, Pallas kernels, local(): pl.pallas_call(density_kernel, grid=(NAUX // rows,), out_shape=(jax.Shape...  9.23 us

profile of v2, /device:TPU:1, one launch (start us, length us, event | category | flops | bytes accessed | tf_op | source)
XLA Modules:
  0.0 102.6 jit_solution(12368954400804657239)
XLA Ops:
  0.6 92.7 %pair_terms.1 = (bf16[2048,512]{1,0:T(8,128)(2,1)}, bf16[2048,512]{1,0:T(8,128)(2,1)}, bf16[2048,512]{1,0:T(8,128)(2,1)}, bf16[2048,512]{1,0:T(8,128)(2,1)}, bf16[2048,512]{1,0:T(8,128)(2,1)}, /*index=5*/f32[1,4]{1,0:T(1,128)}) custom-call(bf16[2048,512]{1,0:T(8,128)(2,1)} %bitcast.3, bf16[2048,128]{1,0:T(8,128)(2,1)} %metric.1, f32[256]{0:T(256)} %occ.1, ...), custom_call_target="tpu_custom_call" | custom-call | tf_op jit(solution)/shard_map/pair_terms/pallas_call | solution.py:309
  93.4 9.2 %density_rows.1 = (f32[8192,128]{1,0:T(8,128)}, f32[1,4]{1,0:T(1,128)}) custom-call(bf16[2048,512]{1,0:T(8,128)(2,1)} %get-tuple-element.10.mine, bf16[2048,512]{1,0:T(8,128)(2,1)} %get-tuple-element.11.sib, bf16[2048,512]{1,0:T(8,128)(2,1)} %get-tuple-element.12.near, bf16[2048,512]{1,0:T(8,128)(2,1)} %get-tuple-element.13.far, ...), custom_call_target="tpu_custom_call" | custom-call | tf_op jit(solution)/shard_map/density_rows/pallas_call | solution.py:350

commit v3 on v2

--- a/solution.py
+++ b/solution.py
@@ -8,7 +8,8 @@
 VISITS = 4
 NAUX = 2048
 NV = 512
-CUTS = ((0, 256), (256, 128), (384, 128))
+CUTS = ((0, 128), (128, 128), (256, 128), (384, 128))
+LAST = len(CUTS) - 1
 SLOT = 72
 MESH = pl.DeviceIdType.MESH
 F32 = jnp.float32
@@ -20,10 +21,10 @@
 
 
 def pair_kernel(
-    raw, metric, occ, virt, mine_out, sib_out, near_out, far_out, tlow_out, energy_out,
-    send, owned, slots, full, mine, sib, near, far, mine_t, coul, amp, vsum, tlow,
+    raw, metric, occ, virt, near_out, far_out, tlow_out, half_out, energy_out,
+    send, owned, near_raw, bounce, slots, full, mine, sib, near, far, mine_t, coul, amp, vsum, tlow, half,
     a2a_s, a2a_r, m1_s, m1_r, mx_s, mx_r, up_s, up_r, down_s, down_r, relay_s, relay_r,
-    sw_s, sw_r, sib_s, sib_r, vis_s, vis_r, far_s, far_r, out_s,
+    sw_s, sw_r, sib_s, sib_r, vis_s, vis_r, far_s, far_r, hop_s, hop_r, out_s,
 ):
     g = lax.axis_index("grp")
     b = lax.axis_index("blk")
@@ -38,6 +39,14 @@
     def chip_core(n):
         return (n // 8, (n % 8) * 2 + c)
 
+    spot = xh * 4 + y
+    gate = 7 - 7 * c
+    crossing = spot == gate
+    landing = ((g + 17 - 2 * c) % 16, 15 * c)
+
+    def at_spot(r):
+        return (g, r * 2 + c)
+
     def at_x(d):
         x2 = (x + d) % 4
         return device(x2 % 2, z, x2 // 2, y, c)
@@ -57,6 +66,17 @@
     partners += [other, chip_core(ahead), chip_core(behind)]
     for partner in partners:
         pl.semaphore_signal(barrier, inc=1, device_id=partner, device_id_type=MESH)
+
+    @pl.when(jnp.logical_not(crossing))
+    def _():
+        pl.semaphore_signal(barrier, inc=1, device_id=at_spot(gate), device_id_type=MESH)
+
+    @pl.when(spot == 7 * c)
+    def _():
+        for r in range(8):
+            pl.semaphore_signal(
+                barrier, inc=1, device_id=((g + 15 + 2 * c) % 16, r * 2 + c), device_id_type=MESH
+            )
 
     order = lax.broadcasted_iota(jnp.int32, (256, 256), 0)
     column = lax.broadcasted_iota(jnp.int32, (256, 256), 1)
@@ -72,17 +92,20 @@
 
     lax.fori_loop(0, 8, relayout, 0)
 
-    pl.semaphore_wait(barrier, len(partners))
+    pl.semaphore_wait(barrier, len(partners) + 1 + jnp.where(crossing, 7, 0))
 
     sends = []
 
-    def push(src, dst, ssem, rsem, to):
+    def launch(src, dst, ssem, rsem, to):
         copy = pltpu.make_async_remote_copy(
             src_ref=src, dst_ref=dst, send_sem=ssem, recv_sem=rsem,
             device_id=to, device_id_type=MESH,
         )
         copy.start()
-        sends.append(copy)
+        return copy
+
+    def push(src, dst, ssem, rsem, to):
+        sends.append(launch(src, dst, ssem, rsem, to))
 
     def arrived(ref, sem):
         pltpu.make_async_copy(ref, ref, sem).wait()
@@ -104,10 +127,42 @@
     land = pl.ds(pl.multiple_of(g * 128, 128), 128)
     for k, (lo, wide) in enumerate(CUTS):
         cut = pl.ds(lo, wide)
-        pltpu.make_async_copy(send.at[g, :, cut], owned.at[land, cut], a2a_r.at[k]).start()
+        dst = owned.at[land, cut]
+        pltpu.make_async_copy(send.at[g, :, cut], dst, a2a_r.at[k]).start()
         for d in range(1, 16):
             to = at_g(d)
-            push(send.at[to[0], :, cut], owned.at[land, cut], a2a_s.at[k, d], a2a_r.at[k], to)
+            push(send.at[to[0], :, cut], dst, a2a_s.at[k, d], a2a_r.at[k], to)
+
+    def chunk(k, rows):
+        cut = pl.ds(*CUTS[k])
+        if k == 0:
+            return owned.at[rows, cut], near_raw.at[rows, :]
+        return mine.at[rows, cut], near.at[rows, cut]
+
+    def eighth(r):
+        return pl.ds(pl.multiple_of(r * 256, 256), 256)
+
+    def forward(k):
+        @pl.when(jnp.logical_not(crossing))
+        def _():
+            src, dst = chunk(k, pl.ds(0, NAUX))
+            launch(src, dst, vis_s.at[k], vis_r.at[k], chip_core(ahead))
+
+        @pl.when(crossing)
+        def _():
+            for n in range(1, 8):
+                r = (gate + n) % 8
+                src, _ = chunk(k, eighth(r))
+                launch(src, bounce.at[k], vis_s.at[k], hop_r.at[k], at_spot(r))
+            src, dst = chunk(k, eighth(gate))
+            launch(src, dst, vis_s.at[k], vis_r.at[k], landing)
+
+    def hop(k):
+        @pl.when(jnp.logical_not(crossing))
+        def _():
+            arrived(bounce.at[k], hop_r.at[k])
+            _, dst = chunk(k, eighth(spot))
+            launch(bounce.at[k], dst, hop_s.at[k], vis_r.at[k], landing)
 
     def piece(py, e):
         px = (x + 4 - e) % 4
@@ -153,9 +208,12 @@
     arrived(piece(above, 0), down_r.at[0])
     arrived(piece(above, 1), down_r.at[1])
     relay_down(2)
+    arrived(owned.at[:, pl.ds(*CUTS[0])], a2a_r.at[0])
+    forward(0)
     hand_over(above, 1)
     arrived(piece(below, 2), up_r.at[2])
     hand_over(below, 2)
+    hop(0)
     opposite = (y + 2) % 4
     for e in (0, 1, 3, 2):
         arrived(piece(opposite, e), relay_r.at[e])
@@ -192,35 +250,55 @@
         copy.start()
         stores.append(copy)
 
-    def visitor(k):
+    def share(src, dst, k, ssem, rsem):
         cut = pl.ds(*CUTS[k])
-        arrived(near.at[:, cut], vis_r.at[k])
-        push(near.at[:, cut], far.at[:, cut], far_s.at[k], far_r.at[k], other)
-
-    for k, (lo, wide) in enumerate(CUTS):
-        cut = pl.ds(lo, wide)
-        arrived(owned.at[:, cut], a2a_r.at[k])
-
-        def fit(q, carry, cut=cut):
+        push(src.at[:, cut], dst.at[:, cut], ssem.at[k], rsem.at[k], other)
+
+    def fit(src, dst, first, size):
+        cut = pl.ds(first, size)
+
+        def step(q, carry):
             at = pl.ds(pl.multiple_of(q * 1024, 1024), 1024)
-            mine[at, cut] = jnp.dot(
-                full[at, :], owned[:, cut], preferred_element_type=F32
+            dst[at, cut] = jnp.dot(
+                full[at, :], src[:, cut], preferred_element_type=F32
             ).astype(BF16)
             return carry
 
-        lax.fori_loop(0, 2, fit, 0)
-        push(mine.at[:, cut], near.at[:, cut], vis_s.at[k], vis_r.at[k], chip_core(ahead))
-        push(mine.at[:, cut], sib.at[:, cut], sib_s.at[k], sib_r.at[k], other)
-
-        def turn(q, carry, lo=lo, wide=wide):
+        lax.fori_loop(0, 2, step, 0)
+
+    def turn(first, size):
+        def step(q, carry):
             at = pl.ds(pl.multiple_of(q * 256, 256), 256)
-            mine_t[pl.ds(lo, wide), at] = mine[at, pl.ds(lo, wide)].T
+            mine_t[pl.ds(first, size), at] = mine[at, pl.ds(first, size)].T
             return carry
 
-        lax.fori_loop(0, 8, turn, 0)
-        if k == 1:
-            visitor(0)
-    keep(mine, mine_out, 0)
+        lax.fori_loop(0, 8, step, 0)
+
+    def visitor(k):
+        _, dst = chunk(k, pl.ds(0, NAUX))
+        arrived(dst, vis_r.at[k])
+        if k == 0:
+            fit(near_raw, near, 0, 128)
+        share(near, far, k, far_s, far_r)
+
+    arrived(owned.at[:, pl.ds(*CUTS[1])], a2a_r.at[1])
+    fit(owned, mine, 0, 256)
+    forward(1)
+    share(mine, sib, 0, sib_s, sib_r)
+    share(mine, sib, 1, sib_s, sib_r)
+    turn(0, 256)
+    hop(1)
+    visitor(0)
+    for k in (2, 3):
+        lo, wide = CUTS[k]
+        arrived(owned.at[:, pl.ds(lo, wide)], a2a_r.at[k])
+        fit(owned, mine, lo, wide)
+        forward(k)
+        share(mine, sib, k, sib_s, sib_r)
+        turn(lo, wide)
+        hop(k)
+        if k == 2:
+            visitor(1)
 
     def orbital(p):
         return (p % 16) * 16 + p // 16
@@ -252,29 +330,36 @@
             total = total + coul[s, at, :] * (2.0 * straight - turned)
             tlow[pl.ds(s * NV + r * 128, 128), :] = (2.0 * turned - straight).astype(BF16)
         energies.append(jnp.sum(total))
-        rows = pl.ds(s * NV, NV)
-        keep(tlow.at[rows, :], tlow_out.at[rows, :], 4 + s)
+        if s >= 2:
+            keep(tlow.at[pl.ds(s * NV, NV), :], tlow_out.at[pl.ds((s - 2) * NV, NV), :], 2 + s)
 
     product(0, mine, 0, NV)
     finish(0)
-    visitor(1)
-    for k, (lo, wide) in enumerate(CUTS):
-        arrived(sib.at[:, pl.ds(lo, wide)], sib_r.at[k])
-    keep(sib, sib_out, 1)
+    visitor(2)
+    for k in range(len(CUTS)):
+        arrived(sib.at[:, pl.ds(*CUTS[k])], sib_r.at[k])
     product(1, sib, 0, NV)
     finish(1)
-    for k in (0, 1):
-        product(2, near, *CUTS[k])
-    for k in (0, 1):
+
+    def resident(q, carry):
+        at = pl.ds(pl.multiple_of(q * 1024, 1024), 1024)
+        value = jnp.dot(mine[at, :], tlow[0:512, :], preferred_element_type=F32)
+        half[at, :] = value + jnp.dot(sib[at, :], tlow[512:1024, :], preferred_element_type=F32)
+        return carry
+
+    lax.fori_loop(0, 2, resident, 0)
+    keep(half, half_out, 0)
+    product(2, near, 0, 256)
+    for k in range(LAST):
         arrived(far.at[:, pl.ds(*CUTS[k])], far_r.at[k])
-        product(3, far, *CUTS[k])
-    visitor(2)
+    product(3, far, 0, 256)
+    visitor(LAST)
     keep(near, near_out, 2)
-    product(2, near, *CUTS[2])
+    product(2, near, 256, 256)
     finish(2)
-    arrived(far.at[:, pl.ds(*CUTS[2])], far_r.at[2])
+    arrived(far.at[:, pl.ds(*CUTS[LAST])], far_r.at[LAST])
     keep(far, far_out, 3)
-    product(3, far, *CUTS[2])
+    product(3, far, 256, 256)
     finish(3)
 
     lane = lax.broadcasted_iota(jnp.int32, (1, VISITS), 1)
@@ -285,15 +370,20 @@
 
     for copy in sends:
         copy.wait_send()
+    for k in range(len(CUTS)):
+        arrived(mine.at[:, pl.ds(*CUTS[k])], vis_s.at[k])
+
+        @pl.when(jnp.logical_not(crossing))
+        def _():
+            arrived(bounce.at[k], hop_s.at[k])
+
     for copy in stores:
         copy.wait()
 
 
-def density_kernel(mine, sib, near, far, tlow, energy, out, energy_out):
-    value = jnp.dot(mine[...], tlow[0:512, :], preferred_element_type=F32)
-    value += jnp.dot(sib[...], tlow[512:1024, :], preferred_element_type=F32)
-    value += jnp.dot(near[...], tlow[1024:1536, :], preferred_element_type=F32)
-    value += jnp.dot(far[...], tlow[1536:2048, :], preferred_element_type=F32)
+def density_kernel(near, far, tlow, half, energy, out, energy_out):
+    value = half[...] + jnp.dot(near[...], tlow[0:512, :], preferred_element_type=F32)
+    value += jnp.dot(far[...], tlow[512:1024, :], preferred_element_type=F32)
     for n in range(4):
         out[pl.ds(n, value.shape[0], stride=4), :] = value[:, n * 128:(n + 1) * 128]
     energy_out[...] = energy[...]
@@ -306,18 +396,21 @@
     n = len(CUTS)
     fits = jax.ShapeDtypeStruct((NAUX, NV), BF16)
     fitted = pltpu.VMEM((NAUX, NV), BF16)
-    mine, sib, near, far, tlow, energy = pl.pallas_call(
+    near, far, tlow, half, energy = pl.pallas_call(
         pair_kernel,
         out_shape=(
-            fits, fits, fits, fits,
-            jax.ShapeDtypeStruct((VISITS * NV, NV), BF16),
+            fits, fits,
+            jax.ShapeDtypeStruct((2 * NV, NV), BF16),
+            jax.ShapeDtypeStruct((NAUX, NV), F32),
             jax.ShapeDtypeStruct((1, VISITS), F32),
         ),
         in_specs=[vmem, hbm, pl.BlockSpec(memory_space=pltpu.SMEM), vmem],
-        out_specs=(hbm, hbm, hbm, hbm, hbm, vmem),
+        out_specs=(hbm, hbm, hbm, hbm, vmem),
         scratch_shapes=[
             pltpu.VMEM((16, 128, NV), BF16),
             fitted,
+            pltpu.VMEM((NAUX, 128), BF16),
+            pltpu.VMEM((n, 256, 128), BF16),
             pltpu.VMEM((16, SLOT, NAUX), BF16),
             pltpu.VMEM((NAUX, NAUX), BF16),
             fitted, fitted, fitted, fitted,
@@ -326,6 +419,7 @@
             pltpu.VMEM((VISITS, NV, NV), F32),
             pltpu.VMEM((NV, NV), F32),
             pltpu.VMEM((VISITS * NV, NV), BF16),
+            pltpu.VMEM((NAUX, NV), F32),
             dma((n, 16)), dma((n,)),
             dma((8, 2)), dma(()),
             dma((4,)), dma((4,)),
@@ -336,6 +430,7 @@
             dma((n,)), dma((n,)),
             dma((n,)), dma((n,)),
             dma((n,)), dma((n,)),
+            dma((n,)), dma((n,)),
             dma((8,)),
         ],
         compiler_params=pltpu.CompilerParams(
@@ -344,7 +439,7 @@
         name="pair_terms",
     )(raw_ints.reshape(NAUX, NV), metric, occ_energy, virt_energy.reshape(1, NV))
 
-    rows = 512
+    rows = 1024
     part = pl.BlockSpec((rows, NV), lambda q: (q, 0))
     small = pl.BlockSpec((1, VISITS), lambda q: (0, 0))
     density, energy = pl.pallas_call(
@@ -354,11 +449,11 @@
             jax.ShapeDtypeStruct((NAUX * NV // 128, 128), F32),
             jax.ShapeDtypeStruct((1, VISITS), F32),
         ),
-        in_specs=[part, part, part, part, pl.BlockSpec((NAUX, NV), lambda q: (0, 0)), small],
+        in_specs=[part, part, pl.BlockSpec((2 * NV, NV), lambda q: (0, 0)), part, small],
         out_specs=(pl.BlockSpec((rows * 4, 128), lambda q: (q, 0)), small),
         compiler_params=pltpu.CompilerParams(vmem_limit_bytes=60 << 20),
         name="density_rows",
-    )(mine, sib, near, far, tlow, energy)
+    )(near, far, tlow, half, energy)
     return density.reshape(NAUX, 1, NV), energy
 
 

time: 103 us -> 100 us (0.971)
  Pallas kernels: 102 us -> 99.6 us
    pallas_call x1, Pallas kernels: 9.23 us -> 6.68 us  [local(): pl.pallas_call(density_kernel, grid=(NAUX // rows,), out_shape=(jax.Shape...]
where the time goes in v3:
time: 100 us
  Pallas kernels  99.6 us (100%)
    pallas_call x1, Pallas kernels, local(): pl.pallas_call(pair_kernel, out_shape=(fits, fits, jax.ShapeDtypeStruct((...  92.9 us
    pallas_call x1, Pallas kernels, local(): pl.pallas_call(density_kernel, grid=(NAUX // rows,), out_shape=(jax.Shape...  6.68 us

profile of v3, /device:TPU:1, one launch (start us, length us, event | category | flops | bytes accessed | tf_op | source)
XLA Modules:
  0.0 100.3 jit_solution(1918763901207401043)
XLA Ops:
  0.6 92.9 %pair_terms.1 = (bf16[2048,512]{1,0:T(8,128)(2,1)}, bf16[2048,512]{1,0:T(8,128)(2,1)}, bf16[1024,512]{1,0:T(8,128)(2,1)}, f32[2048,512]{1,0:T(8,128)}, f32[1,4]{1,0:T(1,128)}) custom-call(bf16[2048,512]{1,0:T(8,128)(2,1)} %bitcast.3, bf16[2048,128]{1,0:T(8,128)(2,1)} %metric.1, f32[256]{0:T(256)} %occ.1, f32[1,512]{1,0:T(1,128)} %bitcast.4), custom_call_target="tpu_custom_call" | custom-call | tf_op jit(solution)/shard_map/pair_terms/pallas_call | solution.py:399
  93.6 6.7 %density_rows.1 = (f32[8192,128]{1,0:T(8,128)}, f32[1,4]{1,0:T(1,128)}) custom-call(bf16[2048,512]{1,0:T(8,128)(2,1)} %get-tuple-element.9.near, bf16[2048,512]{1,0:T(8,128)(2,1)} %get-tuple-element.10.far, bf16[1024,512]{1,0:T(8,128)(2,1)} %get-tuple-element.11.tlow, f32[2048,512]{1,0:T(8,128)} %get-tuple-element.12.half, f32[1,4]{1,0:T(1,128)} %get-tuple-element.13.energy), custom_call_target="tpu_custom_call" | custom-call | tf_op jit(solution)/shard_map/density_rows/pallas_call | solution.py:445

commit v4 on v3

--- a/solution.py
+++ b/solution.py
@@ -156,6 +156,23 @@
                 launch(src, bounce.at[k], vis_s.at[k], hop_r.at[k], at_spot(r))
             src, dst = chunk(k, eighth(gate))
             launch(src, dst, vis_s.at[k], vis_r.at[k], landing)
+
+    def forward_half(k, h):
+        @pl.when(jnp.logical_not(crossing))
+        def _():
+            src, dst = chunk(k, pl.ds(h * 1024, 1024))
+            launch(src, dst, vis_s.at[k], vis_r.at[k], chip_core(ahead))
+
+        for r in range(4 * h, 4 * h + 4):
+            @pl.when(jnp.logical_and(crossing, r != gate))
+            def _():
+                src, _ = chunk(k, eighth(r))
+                launch(src, bounce.at[k], vis_s.at[k], hop_r.at[k], at_spot(r))
+
+            @pl.when(jnp.logical_and(crossing, r == gate))
+            def _():
+                src, dst = chunk(k, eighth(r))
+                launch(src, dst, vis_s.at[k], vis_r.at[k], landing)
 
     def hop(k):
         @pl.when(jnp.logical_not(crossing))
@@ -208,16 +225,16 @@
     arrived(piece(above, 0), down_r.at[0])
     arrived(piece(above, 1), down_r.at[1])
     relay_down(2)
-    arrived(owned.at[:, pl.ds(*CUTS[0])], a2a_r.at[0])
-    forward(0)
     hand_over(above, 1)
     arrived(piece(below, 2), up_r.at[2])
     hand_over(below, 2)
-    hop(0)
     opposite = (y + 2) % 4
     for e in (0, 1, 3, 2):
         arrived(piece(opposite, e), relay_r.at[e])
     hand_over(opposite, 3)
+    arrived(owned.at[:, pl.ds(*CUTS[0])], a2a_r.at[0])
+    forward(0)
+    hop(0)
 
     broad = jnp.broadcast_to(virt[...], (NV, NV))
     vsum[...] = broad + broad.T
@@ -266,6 +283,15 @@
 
         lax.fori_loop(0, 2, step, 0)
 
+    def fit_and_send(k, first, size):
+        cut = pl.ds(first, size)
+        for h in range(2):
+            at = pl.ds(h * 1024, 1024)
+            mine[at, cut] = jnp.dot(
+                full[at, :], owned[:, cut], preferred_element_type=F32
+            ).astype(BF16)
+            forward_half(k, h)
+
     def turn(first, size):
         def step(q, carry):
             at = pl.ds(pl.multiple_of(q * 256, 256), 256)
@@ -282,8 +308,7 @@
         share(near, far, k, far_s, far_r)
 
     arrived(owned.at[:, pl.ds(*CUTS[1])], a2a_r.at[1])
-    fit(owned, mine, 0, 256)
-    forward(1)
+    fit_and_send(1, 0, 256)
     share(mine, sib, 0, sib_s, sib_r)
     share(mine, sib, 1, sib_s, sib_r)
     turn(0, 256)
@@ -292,8 +317,7 @@
     for k in (2, 3):
         lo, wide = CUTS[k]
         arrived(owned.at[:, pl.ds(lo, wide)], a2a_r.at[k])
-        fit(owned, mine, lo, wide)
-        forward(k)
+        fit_and_send(k, lo, wide)
         share(mine, sib, k, sib_s, sib_r)
         turn(lo, wide)
         hop(k)

time: 100 us -> 101 us (1.010)
  Pallas kernels: 99.6 us -> 101 us
where the time goes in v4:
time: 101 us
  Pallas kernels  101 us (100%)
    pallas_call x1, Pallas kernels, local(): pl.pallas_call(pair_kernel, out_shape=(fits, fits, jax.ShapeDtypeStruct((...  93.9 us
    pallas_call x1, Pallas kernels, local(): pl.pallas_call(density_kernel, grid=(NAUX // rows,), out_shape=(jax.Shape...  6.68 us

profile of v4, /device:TPU:1, one launch (start us, length us, event | category | flops | bytes accessed | tf_op | source)
XLA Modules:
  0.0 101.3 jit_solution(5815131924979344349)
XLA Ops:
  0.6 93.9 %pair_terms.1 = (bf16[2048,512]{1,0:T(8,128)(2,1)}, bf16[2048,512]{1,0:T(8,128)(2,1)}, bf16[1024,512]{1,0:T(8,128)(2,1)}, f32[2048,512]{1,0:T(8,128)}, f32[1,4]{1,0:T(1,128)}) custom-call(bf16[2048,512]{1,0:T(8,128)(2,1)} %bitcast.3, bf16[2048,128]{1,0:T(8,128)(2,1)} %metric.1, f32[256]{0:T(256)} %occ.1, f32[1,512]{1,0:T(1,128)} %bitcast.4), custom_call_target="tpu_custom_call" | custom-call | tf_op jit(solution)/shard_map/pair_terms/pallas_call | solution.py:423
  94.6 6.7 %density_rows.1 = (f32[8192,128]{1,0:T(8,128)}, f32[1,4]{1,0:T(1,128)}) custom-call(bf16[2048,512]{1,0:T(8,128)(2,1)} %get-tuple-element.9.near, bf16[2048,512]{1,0:T(8,128)(2,1)} %get-tuple-element.10.far, bf16[1024,512]{1,0:T(8,128)(2,1)} %get-tuple-element.11.tlow, f32[2048,512]{1,0:T(8,128)} %get-tuple-element.12.half, f32[1,4]{1,0:T(1,128)} %get-tuple-element.13.energy), custom_call_target="tpu_custom_call" | custom-call | tf_op jit(solution)/shard_map/density_rows/pallas_call | solution.py:469
